TPU v7x, 128 devices: a whole 4x4x4 slice. The times are simulated.
128 devices in a mesh: row: 8 (over x_lo, z), col: 16 (over x_hi, y, core).
Axes of the slice: x: 4 (x_hi: 2, x_lo: 2; x = x_hi * 2 + x_lo), y: 4, z: 4, core: 2. Of those that a mesh axis runs over, the one named last changes fastest.
Arguments:
- tokens: bfloat16 [2048, 4096], P('row', 'col'), may hold values from -6 to 6
- norm_gain: float32 [4096], replicated, may hold values from 0.1 to 1.9
- expert_ids: int32 [2048, 2], P('row'), may hold values from 0 to 7, all different within a row; in each aligned block of 256 rows (0 to 255, 256 to 511, ...) at most 128 rows name the same one
- gate_weights: float32 [2048, 2], P('row'), may hold values from 0.1 to 1
- w_gate: bfloat16 [8, 4096, 14336], P('row', None, 'col'), may hold values from -0.09375 to 0.09375
- w_up: bfloat16 [8, 4096, 14336], P('row', None, 'col'), may hold values from -0.09375 to 0.09375
- w_down: bfloat16 [8, 14336, 4096], P('row', 'col'), may hold values from -0.046875 to 0.046875
Outputs:
- layer_output: bfloat16 [2048, 4096], P('row', 'col')
Inputs may be any that keep to these rules, and one draw needn't show every extreme that they name: `expert_ids`: the 2 experts of a token differ. In each aligned block of 256 tokens no expert is chosen by more than 128 tokens, a bound that some block reaches.
All inputs are finite; a program needn't handle non-finite values.
Results may differ from a plain program's by a relative error of at most 0.0043.
Values may be sent and summed in bfloat16 or wider, within the bound.
A program may use at most 128 MiB of HBM per device.

v0:
```python
import jax
import jax.numpy as jnp
from jax import lax
from jax.sharding import PartitionSpec as P

EXPERTS = 8
CAP = 128


def normalize(rows, norm_gain):
    values = rows.astype(jnp.float32)
    inverse_norm = lax.rsqrt(jnp.mean(values * values, axis=-1, keepdims=True) + 1e-05)
    return (values * inverse_norm * norm_gain).astype(jnp.bfloat16)


def route_tables(expert_ids, expert_count, capacity):
    token_count = expert_ids.shape[0]
    flat_ids = expert_ids.reshape(-1)
    expert_range = jnp.arange(expert_count, dtype=jnp.int32)
    expert_hits = (flat_ids[:, None] == expert_range[None, :]).astype(jnp.int32)
    earlier = jnp.cumsum(expert_hits, axis=0) - expert_hits
    ranks = jnp.sum(earlier * expert_hits, axis=1)
    slot_index = (flat_ids * capacity + ranks).reshape(token_count, -1)
    slot_ids = jnp.arange(expert_count * capacity, dtype=jnp.int32)
    matches = (slot_index[:, :, None] == slot_ids[None, None, :]).astype(jnp.float32)
    picker = jnp.sum(matches, axis=1)
    return (picker.astype(jnp.bfloat16), slot_index)


def combine_rows(slot_rows, slot_index, gate_weights):
    picked = slot_rows[slot_index]
    return jnp.sum(picked * gate_weights[:, :, None], axis=1)


def run_experts(normed, gate_block, up_block, down_block):
    local_count = gate_block.shape[0]
    sources = normed.shape[0] // local_count
    grouped = normed.reshape(sources, local_count, normed.shape[1], normed.shape[2])
    gate_part = jnp.einsum(
        "slcd,ldf->slcf", grouped, gate_block, preferred_element_type=jnp.float32
    )
    up_part = jnp.einsum("slcd,ldf->slcf", grouped, up_block, preferred_element_type=jnp.float32)
    hidden = (jax.nn.silu(gate_part) * up_part).astype(jnp.bfloat16)
    outputs = jnp.einsum("slcf,lfd->slcd", hidden, down_block, preferred_element_type=jnp.float32)
    return outputs.reshape(normed.shape[0], normed.shape[1], down_block.shape[2])


def body(tokens, norm_gain, expert_ids, gate_weights, w_gate, w_up, w_down):
    picker, slot_index = route_tables(expert_ids, EXPERTS, CAP)
    packed = jnp.einsum("ts,td->sd", picker, tokens, preferred_element_type=jnp.float32).astype(
        jnp.bfloat16
    )
    packed = packed.reshape(EXPERTS, CAP, tokens.shape[1])
    arrived = lax.all_to_all(packed, "row", split_axis=0, concat_axis=0, tiled=True)
    widened = lax.all_gather(arrived, "col", axis=2, tiled=True)
    normed = normalize(widened, norm_gain)
    outputs = run_experts(normed, w_gate, w_up, w_down)
    shares = lax.psum_scatter(outputs, "col", scatter_dimension=2, tiled=True)
    returned = lax.all_to_all(shares, "row", split_axis=0, concat_axis=0, tiled=True)
    mixed = combine_rows(returned.reshape(-1, shares.shape[2]), slot_index, gate_weights)
    return (tokens.astype(jnp.float32) + mixed).astype(jnp.bfloat16)


def solution(mesh):
    placed = (
        P("row", "col"),
        P(),
        P("row", None),
        P("row", None),
        P("row", None, "col"),
        P("row", None, "col"),
        P("row", "col", None),
    )
    return jax.shard_map(
        body, mesh=mesh, in_specs=placed, out_specs=P("row", "col"), check_vma=False
    )
```

profile of v0, /device:TPU:0, one launch (start us, length us, event | category | flops | bytes accessed | tf_op | source)
XLA Modules:
  0.0 323.9 jit_solution(4479239125791643411)
XLA Ops:
  6.5 0.8 copy.21
  7.4 0.1 eq.42
  7.5 0.1 eq.38
  7.7 1.1 reduce-window.6
  8.8 0.2 slice_reduce_fusion
  9.1 0.1 fusion.30
  9.2 0.1 reduce_sum.39
  9.3 0.1 copy.23
  9.4 0.7 compare_select_fusion
  10.1 0.3 convert_reduce_fusion
  10.4 1.3 convolution_convert_fusion
  11.6 16.3 %all_to_all.10 = bf16[8,128,256]{2,1,0:T(8,128)(2,1)} all-to-all(bf16[8,128,256]{2,1,0:T(8,128)(2,1)S(1)} %bitcast.67), channel_id=1, replica_groups=mesh['row'=8,'col'=16] {'row'}, dimensions={0} | all-to-all | bytes 1048576 | tf_op jit(solution)/shard_map/all_to_all | solution.py:54
  27.9 0.0 all-gather.2.cloned.1.call-update
  27.9 0.0 reduce-scatter.2.cloned.1.call-start
  28.0 76.0 %all-gather.2.cloned.1.call-done = bf16[8,128,4096]{2,1,0:T(8,128)(2,1)} async-done(((bf16[8,128,256]{2,1,0:T(8,128)(2,1)}), bf16[8,128,4096]{2,1,0:T(8,128)(2,1)}) %all-gather.2.cloned.1.call-update) | async-done | bytes 8388624 | tf_op jit(solution)/shard_map/all_gather | solution.py:55
  104.0 5.2 %fusion = f32[8,128]{1,0:T(8,128)S(1)} fusion(bf16[8,128,4096]{2,1,0:T(8,128)(2,1)} %all-gather.2.cloned.1.call-done), kind=kLoop, calls=%fused_computation.3 | loop fusion | flops 12581888 | bytes 8392704 | tf_op jit(solution)/shard_map/reduce_sum | solution.py:12
  109.3 0.5 copy-done
  109.8 12.5 %fusion.7 = f32[8,128,896]{2,1,0:T(8,128)} fusion(bf16[1,4096,896]{2,1,0:T(8,128)(2,1)} %param.11, bf16[8,128,4096]{2,1,0:T(8,128)(2,1)S(1)} %copy-done, f32[4096]{0:T(1024)S(1)} %copy-done.3, f32[8,128]{1,0:T(8,128)S(1)} %add_rsqrt_fusion), kind=kOutput, calls=%fused_computation.10 | convolution fusion | flops 7532969984 | bytes 19419136 | tf_op jit(solution)/shard_map/slcd,ldf->slcf/dot_general | solution.py:39
  122.3 28.0 %fusion.3 = f32[8,128,4096]{2,1,0:T(8,128)} fusion(bf16[1,896,4096]{2,1,0:T(8,128)(2,1)} %param.13, f32[8,128,896]{2,1,0:T(8,128)} %fusion.7, bf16[1,4096,896]{2,1,0:T(8,128)(2,1)} %param.12, bf16[8,128,4096]{2,1,0:T(8,128)(2,1)} %all-gather.2.cloned.1.call-done, f32[4096]{0:T(1024)S(1)} %copy-done.3, f32[8,128]{1,0:T(8,128)S(1)} %add_rsqrt_fusion), kind=kOutput, calls=%fused_computation.6 | convolution fusion | flops 15054667776 | bytes 43536384 | tf_op jit(solution)/shard_map/slcf,lfd->slcd/dot_general | solution.py:44
  150.4 0.0 reduce-scatter.2.cloned.1.call-update
  150.4 0.0 copy-start.1
  150.4 144.8 %reduce-scatter.2.cloned.1.call-done = f32[8,128,256]{2,1,0:T(8,128)} async-done(((f32[8,128,4096]{2,1,0:T(8,128)}), f32[8,128,256]{2,1,0:T(8,128)}) %reduce-scatter.2.cloned.1.call-update) | async-done | bytes 1048592 | tf_op jit(solution)/shard_map/reduce_scatter | solution.py:58
  295.2 4.4 %all-to-all-start.1 = ((f32[8,128,256]{2,1,0:T(8,128)}), f32[8,128,256]{2,1,0:T(8,128)S(1)}, u32[]{:S(2)}, u32[]{:S(2)}) async-start(f32[8,128,256]{2,1,0:T(8,128)} %reduce-scatter.2.cloned.1.call-done), calls=%async_computation.2 | async-start | bytes 2097152 | tf_op jit(solution)/shard_map/all_to_all | solution.py:59
  299.6 0.1 copy.24
  299.7 0.1 reshape.72
  299.9 0.1 copy.25
  300.1 13.7 %all-to-all-done.1 = f32[8,128,256]{2,1,0:T(8,128)S(1)} async-done(((f32[8,128,256]{2,1,0:T(8,128)}), f32[8,128,256]{2,1,0:T(8,128)S(1)}, u32[]{:S(2)}, u32[]{:S(2)}) %all-to-all-start.1) | async-done | bytes 1048608 | tf_op jit(solution)/shard_map/all_to_all | solution.py:59
  313.8 1.6 gather_fusion
  315.4 0.3 reshape.71
  315.7 0.7 multiply_reduce_fusion
  316.4 0.0 copy-done.1
  316.4 0.7 add_convert_fusion
  (11 shorter events, 0.1 us)
Async XLA Ops:
  6.5 102.7 %copy-start.3 = (f32[4096]{0:T(1024)S(1)}, f32[4096]{0:T(1024)}, u32[]{:S(2)}) copy-start(f32[4096]{0:T(1024)} %param.8) | copy-start | bytes 49156
  6.5 97.5 %all-gather.2.cloned.1.call-start = ((), (), s32[]{:S(2)}) async-start(), calls=%async_computation.3 | async-start | bytes 8912896 | tf_op jit(solution)/shard_map/all_gather | solution.py:55
  27.9 267.2 %reduce-scatter.2.cloned.1.call-start = ((), (), s32[]{:S(2)}) async-start(), calls=%async_computation.4 | async-start | bytes 17825792 | tf_op jit(solution)/shard_map/reduce_scatter | solution.py:58
  104.0 5.8 %copy-start = (bf16[8,128,4096]{2,1,0:T(8,128)(2,1)S(1)}, bf16[8,128,4096]{2,1,0:T(8,128)(2,1)}, u32[]{:S(2)}) copy-start(bf16[8,128,4096]{2,1,0:T(8,128)(2,1)} %all-gather.2.cloned.1.call-done) | copy-start | bytes 25165828
  150.4 149.5 %copy-start.2 = (f32[256,2]{0,1:T(2,128)S(1)}, f32[256,2]{0,1:T(2,128)}, u32[]{:S(2)}) copy-start(f32[256,2]{0,1:T(2,128)} %param.10) | copy-start | bytes 6148
  150.4 166.0 %copy-start.1 = (bf16[256,256]{1,0:T(8,128)(2,1)S(1)}, bf16[256,256]{1,0:T(8,128)(2,1)}, u32[]{:S(2)}) copy-start(bf16[256,256]{1,0:T(8,128)(2,1)} %param.7) | copy-start | bytes 393220
  295.2 18.6 %all-to-all-start.1 = ((f32[8,128,256]{2,1,0:T(8,128)}), f32[8,128,256]{2,1,0:T(8,128)S(1)}, u32[]{:S(2)}, u32[]{:S(2)}) async-start(f32[8,128,256]{2,1,0:T(8,128)} %reduce-scatter.2.cloned.1.call-done), calls=%async_computation.2 | async-start | bytes 2097152 | tf_op jit(solution)/shard_map/all_to_all | solution.py:59
Sparse Core Ops, SparseCore 0:
  28.1 75.9 all-gather.1
  150.5 144.6 reduce-scatter.1
where the time goes:
time: 324 us
  waiting for transfers between devices  235 us (73%)
  matrix products  41.8 us (13%)
  blocking collectives  16.3 us (5%)
  between operations  13.5 us (4%)
  other arithmetic  8.85 us (3%)
  starting transfers between devices  4.49 us (1%)
  local copies, waits for them, and re-layouts  4.36 us (1%)
    reduce_scatter x1, waiting for transfers between devices, body(): shares = lax.psum_scatter(outputs, 'col', scatter_dimension=2, tiled=True)  145 us
    all_gather x1, waiting for transfers between devices, body(): widened = lax.all_gather(arrived, 'col', axis=2, tiled=True)  76 us
    dot_general x1, matrix products, run_experts(): jnp.einsum('slcf,lfd->slcd', hidden, down_block, preferred_element_type=j...  28 us
    all_to_all x1, blocking collectives, body(): lax.all_to_all(packed, 'row', split_axis=0, concat_axis=0, tiled=True)  16.3 us
    all_to_all x1, waiting for transfers between devices, body(): lax.all_to_all(shares, 'row', split_axis=0, concat_axis=0, tiled=True)  13.7 us
    dot_general x1, matrix products, run_experts(): jnp.einsum('slcd,ldf->slcf', grouped, gate_block, preferred_element_type=...  12.5 us
  transfers between devices with their start and end apart: 3, of which 3 were waited for; matrix products, arithmetic and copies ran while one was open for 0% of the time, Pallas kernels for 0%

commit v1 on v0

--- a/solution.py
+++ b/solution.py
@@ -52,7 +52,9 @@
     )
     packed = packed.reshape(EXPERTS, CAP, tokens.shape[1])
     arrived = lax.all_to_all(packed, "row", split_axis=0, concat_axis=0, tiled=True)
-    widened = lax.all_gather(arrived, "col", axis=2, tiled=True)
+    widened = jnp.concatenate(
+        lax.all_to_all(jnp.stack([arrived] * lax.axis_size("col")), "col", 0, 0), axis=2
+    )
     normed = normalize(widened, norm_gain)
     outputs = run_experts(normed, w_gate, w_up, w_down)
     shares = lax.psum_scatter(outputs, "col", scatter_dimension=2, tiled=True)

time: 324 us -> 405 us (1.25)
  waiting for transfers between devices: 235 us -> 288 us
  local copies, waits for them, and re-layouts: 4.36 us -> 23.3 us
  starting transfers between devices: 4.49 us -> 11.6 us
    all_to_all x0 -> x1, waiting for transfers between devices: none -> 120 us  [body(): lax.all_to_all(jnp.stack([arrived] * lax.axis_size('col')), 'col', 0, 0)]
    all_gather x1 -> x0, waiting for transfers between devices: 76 us -> none  [body(): widened = lax.all_gather(arrived, 'col', axis=2, tiled=True)]
    all_to_all x0 -> x1, local copies, waits for them, and re-layouts: none -> 11.4 us  [body(): lax.all_to_all(jnp.stack([arrived] * lax.axis_size('col')), 'col', 0, 0)]
    reduce_scatter x1, waiting for transfers between devices: 145 us -> 154 us  [body(): shares = lax.psum_scatter(outputs, 'col', scatter_dimension=2, tiled=True)]
    all_to_all x0 -> x1, starting transfers between devices: none -> 6.92 us  [body(): lax.all_to_all(jnp.stack([arrived] * lax.axis_size('col')), 'col', 0, 0)]
    another operation x1 -> x2, local copies, waits for them, and re-layouts: 0.01 us -> 4.26 us  [the longest x1 4.26 us: body(): jnp.stack([arrived] * lax.axis_size('col'))]
where the time goes in v1:
time: 405 us
  waiting for transfers between devices  288 us (71%)
  matrix products  40.4 us (10%)
  local copies, waits for them, and re-layouts  23.3 us (6%)
  blocking collectives  16.2 us (4%)
  between operations  13.6 us (3%)
  other arithmetic  11.8 us (3%)
  starting transfers between devices  11.6 us (3%)
    reduce_scatter x1, waiting for transfers between devices, body(): shares = lax.psum_scatter(outputs, 'col', scatter_dimension=2, tiled=True)  154 us
    all_to_all x1, waiting for transfers between devices, body(): lax.all_to_all(jnp.stack([arrived] * lax.axis_size('col')), 'col', 0, 0)  120 us
    dot_general x1, matrix products, run_experts(): jnp.einsum('slcf,lfd->slcd', hidden, down_block, preferred_element_type=j...  28.1 us
    all_to_all x1, blocking collectives, body(): lax.all_to_all(packed, 'row', split_axis=0, concat_axis=0, tiled=True)  16.2 us
    all_to_all x1, waiting for transfers between devices, body(): lax.all_to_all(shares, 'row', split_axis=0, concat_axis=0, tiled=True)  13.8 us
    all_to_all x1, local copies, waits for them, and re-layouts, body(): lax.all_to_all(jnp.stack([arrived] * lax.axis_size('col')), 'col', 0, 0)  11.4 us
    dot_general x1, matrix products, run_experts(): jnp.einsum('slcd,ldf->slcf', grouped, gate_block, preferred_element_type=...  11 us
  transfers between devices with their start and end apart: 3, of which 3 were waited for; matrix products, arithmetic and copies ran while one was open for 0% of the time, Pallas kernels for 0%

profile of v1, /device:TPU:0, one launch (start us, length us, event | category | flops | bytes accessed | tf_op | source)
XLA Modules:
  0.0 404.6 jit_solution(4523859034384932434)
XLA Ops:
  6.5 0.8 copy.37
  7.3 0.1 eq.42
  7.5 0.1 eq.38
  7.7 1.1 reduce-window.6
  8.8 0.2 slice_reduce_fusion
  9.1 0.1 fusion.23
  9.1 0.1 reduce_sum.39
  9.4 0.7 compare_select_fusion
  10.1 0.3 convert_reduce_fusion
  10.3 1.3 convolution_convert_fusion
  11.6 16.2 %all_to_all.15 = bf16[8,128,256]{2,1,0:T(8,128)(2,1)S(1)} all-to-all(bf16[8,128,256]{2,1,0:T(8,128)(2,1)S(1)} %bitcast.74), channel_id=1, replica_groups=mesh['row'=8,'col'=16] {'row'}, dimensions={0} | all-to-all | bytes 1048576 | tf_op jit(solution)/shard_map/all_to_all | solution.py:54
  27.8 4.3 %stack.2 = bf16[16,8,128,256]{3,2,1,0:T(8,128)(2,1)} broadcast(bf16[8,128,256]{2,1,0:T(8,128)(2,1)S(1)} %all_to_all.15), dimensions={1,2,3} | broadcast | bytes 8912896 | tf_op jit(solution)/shard_map/stack | solution.py:56
  32.1 6.9 %all-to-all-start.1 = ((bf16[16,8,128,256]{3,2,1,0:T(8,128)(2,1)}), bf16[16,8,128,256]{3,2,1,0:T(8,128)(2,1)}, u32[]{:S(2)}, u32[]{:S(2)}) async-start(bf16[16,8,128,256]{3,2,1,0:T(8,128)(2,1)} %stack.2), calls=%async_computation.1 | async-start | bytes 16777216 | tf_op jit(solution)/shard_map/all_to_all | solution.py:56
  39.0 0.2 reduce-scatter.2.cloned.1.call-start
  39.2 119.8 %all-to-all-done.1 = bf16[16,8,128,256]{3,2,1,0:T(8,128)(2,1)} async-done(((bf16[16,8,128,256]{3,2,1,0:T(8,128)(2,1)}), bf16[16,8,128,256]{3,2,1,0:T(8,128)(2,1)}, u32[]{:S(2)}, u32[]{:S(2)}) %all-to-all-start.1) | async-done | bytes 8388640 | tf_op jit(solution)/shard_map/all_to_all | solution.py:56
  159.1 11.4 %copy.40 = bf16[16,8,128,256]{2,3,0,1:T(8,128)(2,1)} copy(bf16[16,8,128,256]{3,2,1,0:T(8,128)(2,1)} %all-to-all-done.1) | data formatting | bytes 16777216 | tf_op jit(solution)/shard_map/all_to_all | solution.py:56
  170.5 5.2 %fusion = f32[8,128]{1,0:T(8,128)S(1)} fusion(bf16[16,8,128,256]{2,3,0,1:T(8,128)(2,1)} %copy.40), kind=kLoop, calls=%fused_computation.3 | loop fusion | flops 12581888 | bytes 8392704 | tf_op jit(solution)/shard_map/reduce_sum | solution.py:12
  175.7 0.6 copy-done
  176.3 3.0 fusion.2
  179.3 3.2 copy-done.1
  182.5 11.0 %fusion.7 = f32[8,128,896]{2,1,0:T(8,128)} fusion(bf16[8,128,4096]{1,2,0:T(8,128)(2,1)S(1)} %bitcast.71, bf16[1,4096,896]{2,1,0:T(8,128)(2,1)S(1)} %bitcast.76), kind=kOutput, calls=%fused_computation.10 | convolution fusion | flops 7516192768 | bytes 19398656 | tf_op jit(solution)/shard_map/slcd,ldf->slcf/dot_general | solution.py:39
  193.5 28.1 %fusion.3 = f32[8,128,4096]{2,1,0:T(8,128)} fusion(bf16[1,896,4096]{2,1,0:T(8,128)(2,1)} %param.13, f32[8,128,896]{2,1,0:T(8,128)} %fusion.7, bf16[8,128,4096]{1,2,0:T(8,128)(2,1)} %bitcast.72, bf16[1,4096,896]{2,1,0:T(8,128)(2,1)} %param.12), kind=kOutput, calls=%fused_computation.6 | convolution fusion | flops 15037890560 | bytes 43515904 | tf_op jit(solution)/shard_map/slcf,lfd->slcd/dot_general | solution.py:44
  221.7 154.1 %reduce-scatter.2.cloned.1.call-done = f32[8,128,256]{2,1,0:T(8,128)} async-done(((f32[8,128,4096]{2,1,0:T(8,128)}), f32[8,128,256]{2,1,0:T(8,128)}) %reduce-scatter.2.cloned.1.call-update) | async-done | bytes 1048592 | tf_op jit(solution)/shard_map/reduce_scatter | solution.py:60
  375.8 4.4 %all-to-all-start.2 = ((f32[8,128,256]{2,1,0:T(8,128)}), f32[8,128,256]{2,1,0:T(8,128)S(1)}, u32[]{:S(2)}, u32[]{:S(2)}) async-start(f32[8,128,256]{2,1,0:T(8,128)} %reduce-scatter.2.cloned.1.call-done), calls=%async_computation.3 | async-start | bytes 2097152 | tf_op jit(solution)/shard_map/all_to_all | solution.py:61
  380.2 0.1 copy.43
  380.3 0.1 reshape.82
  380.5 0.1 copy.44
  380.7 13.8 %all-to-all-done.2 = f32[8,128,256]{2,1,0:T(8,128)S(1)} async-done(((f32[8,128,256]{2,1,0:T(8,128)}), f32[8,128,256]{2,1,0:T(8,128)S(1)}, u32[]{:S(2)}, u32[]{:S(2)}) %all-to-all-start.2) | async-done | bytes 1048608 | tf_op jit(solution)/shard_map/all_to_all | solution.py:61
  394.4 1.6 gather_fusion
  396.0 0.3 reshape.81
  396.3 0.7 multiply_reduce_fusion
  397.0 0.7 add_convert_fusion
  (21 shorter events, 0.2 us)
Async XLA Ops:
  32.1 7.2 %copy-start.3 = (f32[4096]{0:T(1024)S(1)}, f32[4096]{0:T(1024)}, u32[]{:S(2)}) copy-start(f32[4096]{0:T(1024)} %param.8) | copy-start | bytes 49156
  32.1 127.0 %all-to-all-start.1 = ((bf16[16,8,128,256]{3,2,1,0:T(8,128)(2,1)}), bf16[16,8,128,256]{3,2,1,0:T(8,128)(2,1)}, u32[]{:S(2)}, u32[]{:S(2)}) async-start(bf16[16,8,128,256]{3,2,1,0:T(8,128)(2,1)} %stack.2), calls=%async_computation.1 | async-start | bytes 16777216 | tf_op jit(solution)/shard_map/all_to_all | solution.py:56
  39.0 336.8 %reduce-scatter.2.cloned.1.call-start = ((), (), s32[]{:S(2)}) async-start(), calls=%async_computation.4 | async-start | bytes 17825792 | tf_op jit(solution)/shard_map/reduce_scatter | solution.py:60
  170.5 5.8 %copy-start = (bf16[16,8,128,256]{2,3,0,1:T(8,128)(2,1)S(1)}, bf16[16,8,128,256]{2,3,0,1:T(8,128)(2,1)}, u32[]{:S(2)}) copy-start(bf16[16,8,128,256]{2,3,0,1:T(8,128)(2,1)} %copy.40) | copy-start | bytes 25165828
  170.5 12.0 %slice-start = ((s8[7340032]{0:T(1024)(128)(4,1)}), s8[3145728]{0:T(1024)(128)(4,1)S(1)}, s32[]{:S(2)}) async-start(s8[7340032]{0:T(1024)(128)(4,1)} %bitcast.75), calls=%async_computation.5 | async-start | bytes 6291456
  176.3 6.2 %slice-start.1 = ((s8[7340032]{0:T(1024)(128)(4,1)}), s8[4194304]{0:T(1024)(128)(4,1)S(1)}, s32[]{:S(2)}) async-start(s8[7340032]{0:T(1024)(128)(4,1)} %bitcast.75), calls=%async_computation.6 | async-start | bytes 8388608
  179.3 3.2 copy-start.1
  221.6 158.9 %copy-start.4 = (f32[256,2]{0,1:T(2,128)S(1)}, f32[256,2]{0,1:T(2,128)}, u32[]{:S(2)}) copy-start(f32[256,2]{0,1:T(2,128)} %param.10) | copy-start | bytes 6148
  221.7 175.4 %copy-start.2 = (bf16[256,256]{1,0:T(8,128)(2,1)S(1)}, bf16[256,256]{1,0:T(8,128)(2,1)}, u32[]{:S(2)}) copy-start(bf16[256,256]{1,0:T(8,128)(2,1)} %param.7) | copy-start | bytes 393220
  375.8 18.7 %all-to-all-start.2 = ((f32[8,128,256]{2,1,0:T(8,128)}), f32[8,128,256]{2,1,0:T(8,128)S(1)}, u32[]{:S(2)}, u32[]{:S(2)}) async-start(f32[8,128,256]{2,1,0:T(8,128)} %reduce-scatter.2.cloned.1.call-done), calls=%async_computation.3 | async-start | bytes 2097152 | tf_op jit(solution)/shard_map/all_to_all | solution.py:61
Sparse Core Ops, SparseCore 0:
  221.8 153.9 reduce-scatter.1
